TPU v7x, 1024 devices: a whole 4x8x16 slice. The times are simulated.
1024 devices in a mesh: expert: 32 (over x, y), cuts: 2 (over core), dp: 16 (over z).
Axes of the slice: x: 4, y: 8, z: 16, core: 2. Of those that a mesh axis runs over, the one named last changes fastest.
Arguments:
- activations: bfloat16 [65536, 2048], P(('expert', 'dp')), may hold values from -6 to 6
- out_grad: bfloat16 [65536, 2048], P(('expert', 'dp')), may hold values from -6 to 6
- expert_ids: int32 [65536, 1], P(('expert', 'dp')), may hold values from 0 to 31; in each aligned block of 128 rows (0 to 127, 128 to 255, ...) at most 5 rows name the same one
- gate_up_weight: bfloat16 [32, 2048, 2, 768], P('expert', None, None, 'cuts'), may hold values from -0.125 to 0.125
- down_weight: bfloat16 [32, 2048, 768], P('expert', None, 'cuts'), may hold values from -0.21875 to 0.21875
- master_weight: float32 [32, 2048, 3, 768], P('expert', 'dp', None, 'cuts'), may hold values from -6 to 6
- first_moment: bfloat16 [32, 2048, 3, 768], P('expert', 'dp', None, 'cuts'), may hold values from -6 to 6
- second_moment: bfloat16 [32, 2048, 3, 768], P('expert', 'dp', None, 'cuts'), may hold values from 0.5 to 8
- new_owner: int32 [32, 32], replicated, may hold values from 0 to 31, each once within a row
Outputs:
- input_grad: bfloat16 [65536, 2048], P(('expert', 'dp'), 'cuts')
- moved_master: float32 [32, 32, 64, 3, 768], P('expert', None, 'dp', None, 'cuts')
- moved_first: bfloat16 [32, 32, 64, 3, 768], P('expert', None, 'dp', None, 'cuts')
- moved_second: bfloat16 [32, 32, 64, 3, 768], P('expert', None, 'dp', None, 'cuts')
Inputs may be any that keep to these rules, and one draw needn't show every extreme that they name: `expert_ids`: within the 128 rows of one device no expert is named by more than 5 rows, and in every draw some device names some expert exactly 5 times. `new_owner`: each row names every owner index exactly once.
All inputs are finite; a program needn't handle non-finite values.
Results may differ from a plain program's by a relative error of at most 0.019.
Values may be sent and summed in bfloat16 or wider, within the bound.
A program may use at most 64 MiB of HBM per device.

v0:
```python
import jax
import jax.numpy as jnp
from jax import lax
from jax.sharding import PartitionSpec as P

beta_first = 0.9
beta_second = 0.95
learn_rate = 0.01
decay_rate = 0.1
epsilon = 1e-08


def adam_update(master, first_old, second_old, gradient):
    first_new = beta_first * first_old.astype(jnp.float32) + (1.0 - beta_first) * gradient
    second_new = (
        beta_second * second_old.astype(jnp.float32) + (1.0 - beta_second) * gradient * gradient
    )
    master_new = master - learn_rate * (
        first_new / (jnp.sqrt(second_new) + epsilon) + decay_rate * master
    )
    return (master_new, first_new, second_new)


def local(
    activations,
    out_grad,
    expert_ids,
    gate_up_weight,
    down_weight,
    master_weight,
    first_moment,
    second_moment,
    new_owner,
):
    experts = lax.axis_size("expert")
    dp_count = lax.axis_size("dp")
    row_count = activations.shape[0]
    model_width = activations.shape[1]
    capacity = row_count // experts + max(1, row_count // (4 * experts))
    shard_rows = model_width // dp_count
    slice_rows = shard_rows // experts
    unit_count = master_weight.shape[3]
    expert_index = lax.axis_index("expert")
    owners = lax.dynamic_slice_in_dim(new_owner, expert_index, 1, 0)[0]
    send_order = jnp.argsort(owners)

    def arrange(tensor):
        return jnp.take(tensor.reshape(experts, slice_rows, 3, unit_count), send_order, axis=0)

    row_expert = expert_ids[:, 0]
    onehot = (row_expert[:, None] == jnp.arange(experts, dtype=jnp.int32)[None, :]).astype(
        jnp.int32
    )
    within = jnp.sum(jnp.cumsum(onehot, axis=0) * onehot, axis=1) - 1
    target = row_expert * capacity + within
    dispatch = (jnp.arange(experts * capacity, dtype=jnp.int32)[:, None] == target[None, :]).astype(
        jnp.bfloat16
    )
    send_in = jnp.dot(dispatch, activations, preferred_element_type=jnp.float32).astype(
        jnp.bfloat16
    )
    send_grad = jnp.dot(dispatch, out_grad, preferred_element_type=jnp.float32).astype(jnp.bfloat16)
    got_in, got_grad = (
        lax.all_to_all(
            send_in.reshape(experts, capacity, model_width),
            "expert",
            split_axis=0,
            concat_axis=0,
            tiled=True,
        ),
        lax.all_to_all(
            send_grad.reshape(experts, capacity, model_width),
            "expert",
            split_axis=0,
            concat_axis=0,
            tiled=True,
        ),
    )
    slots_in = got_in.reshape(experts * capacity, model_width)
    slots_grad = got_grad.reshape(experts * capacity, model_width)
    gate_up = gate_up_weight[0].reshape(model_width, -1)
    projected = jnp.dot(slots_in, gate_up, preferred_element_type=jnp.float32)
    gate_value = projected[:, :unit_count]
    lift_value = projected[:, unit_count:]
    sigmoid_gate = jax.nn.sigmoid(gate_value)
    silu_gate = gate_value * sigmoid_gate
    hidden = (silu_gate * lift_value).astype(jnp.bfloat16)
    hidden_grad = jnp.dot(slots_grad, down_weight[0], preferred_element_type=jnp.float32)
    lift_grad = (hidden_grad * silu_gate).astype(jnp.bfloat16)
    gate_grad = (
        hidden_grad * lift_value * sigmoid_gate * (1.0 + gate_value * (1.0 - sigmoid_gate))
    ).astype(jnp.bfloat16)
    pair_grad = jnp.concatenate([gate_grad, lift_grad], axis=1)
    slot_grad = lax.dot_general(
        pair_grad, gate_up, (((1,), (1,)), ((), ())), preferred_element_type=jnp.float32
    )
    returned = lax.all_to_all(
        slot_grad.astype(jnp.bfloat16).reshape(experts, capacity, model_width),
        "expert",
        split_axis=0,
        concat_axis=0,
        tiled=True,
    )
    row_grad = lax.dot_general(
        dispatch,
        returned.reshape(experts * capacity, model_width),
        (((0,), (0,)), ((), ())),
        preferred_element_type=jnp.float32,
    )
    input_grad = lax.psum_scatter(
        row_grad.astype(jnp.bfloat16), "cuts", scatter_dimension=1, tiled=True
    )
    paired = lax.dot_general(
        slots_in, pair_grad, (((0,), (0,)), ((), ())), preferred_element_type=jnp.float32
    )
    downed = lax.dot_general(
        slots_grad, hidden, (((0,), (0,)), ((), ())), preferred_element_type=jnp.float32
    )
    summed = lax.psum_scatter(
        jnp.concatenate([paired, downed], axis=1).astype(jnp.bfloat16),
        "dp",
        scatter_dimension=0,
        tiled=True,
    ).astype(jnp.float32)
    gradient = summed.reshape(shard_rows, 3, unit_count) / dp_count
    master_new, first_new, second_new = adam_update(
        master_weight[0], first_moment[0], second_moment[0], gradient
    )
    moved_master = lax.all_to_all(
        arrange(master_new).astype(jnp.bfloat16), "expert", split_axis=0, concat_axis=0, tiled=True
    ).astype(jnp.float32)
    moved_first, moved_second = (
        lax.all_to_all(
            arrange(first_new.astype(jnp.bfloat16)),
            "expert",
            split_axis=0,
            concat_axis=0,
            tiled=True,
        ),
        lax.all_to_all(
            arrange(second_new.astype(jnp.bfloat16)),
            "expert",
            split_axis=0,
            concat_axis=0,
            tiled=True,
        ),
    )
    return (input_grad, moved_master[None], moved_first[None], moved_second[None])


def solution(mesh):
    in_specs = (
        P(("expert", "dp"), None),
        P(("expert", "dp"), None),
        P(("expert", "dp"), None),
        P("expert", None, None, "cuts"),
        P("expert", None, "cuts"),
        P("expert", "dp", None, "cuts"),
        P("expert", "dp", None, "cuts"),
        P("expert", "dp", None, "cuts"),
        P(),
    )
    out_specs = (
        P(("expert", "dp"), "cuts"),
        P("expert", None, "dp", None, "cuts"),
        P("expert", None, "dp", None, "cuts"),
        P("expert", None, "dp", None, "cuts"),
    )
    return jax.shard_map(local, mesh=mesh, in_specs=in_specs, out_specs=out_specs, check_vma=False)
```

profile of v0, /device:TPU:8, one launch (start us, length us, event | category | flops | bytes accessed | tf_op | source)
XLA Modules:
  0.0 271.3 jit_solution(4515317326178812026)
XLA Ops:
  13.2 16.6 %all-to-all-start.1 = ((bf16[32,5,2048]{2,1,0:T(8,128)(2,1)}), bf16[32,5,2048]{2,1,0:T(8,128)(2,1)S(1)}, u32[]{:S(2)}, u32[]{:S(2)}) async-start(bf16[32,5,2048]{2,1,0:T(8,128)(2,1)} %reshape.72), calls=%async_computation.1 | async-start | bytes 2097152 | tf_op jit(solution)/shard_map/all_to_all | solution.py:64
  32.4 19.5 %all-to-all-done.1 = bf16[32,5,2048]{2,1,0:T(8,128)(2,1)S(1)} async-done(((bf16[32,5,2048]{2,1,0:T(8,128)(2,1)}), bf16[32,5,2048]{2,1,0:T(8,128)(2,1)S(1)}, u32[]{:S(2)}, u32[]{:S(2)}) %all-to-all-start.1) | async-done | bytes 655392 | tf_op jit(solution)/shard_map/all_to_all | solution.py:64
  51.9 5.2 %all-to-all-start = ((bf16[32,5,2048]{2,1,0:T(8,128)(2,1)}), bf16[32,5,2048]{2,1,0:T(8,128)(2,1)}, u32[]{:S(2)}, u32[]{:S(2)}) async-start(bf16[32,5,2048]{2,1,0:T(8,128)(2,1)} %reshape.70), calls=%async_computation | async-start | bytes 2097152 | tf_op jit(solution)/shard_map/all_to_all | solution.py:71
  57.2 4.2 %copy.50 = bf16[256,8,2,384]{3,1,2,0:T(8,128)(2,1)} copy(bf16[256,8,2,384]{3,2,1,0:T(2,128)(2,1)} %bitcast.41) | data formatting | bytes 6291456
  61.6 2.6 fusion.14
  64.2 14.4 %all-to-all-done = bf16[32,5,2048]{2,1,0:T(8,128)(2,1)} async-done(((bf16[32,5,2048]{2,1,0:T(8,128)(2,1)}), bf16[32,5,2048]{2,1,0:T(8,128)(2,1)}, u32[]{:S(2)}, u32[]{:S(2)}) %all-to-all-start) | async-done | bytes 655392 | tf_op jit(solution)/shard_map/all_to_all | solution.py:71
  78.6 1.5 reshape.71
  82.3 2.6 pad_maximum_fusion
  84.9 6.8 %copy.48 = bf16[2048,1152]{1,0:T(8,128)(2,1)} copy(bf16[2048,1152]{0,1:T(8,128)(2,1)} %pad_maximum_fusion) | data formatting | bytes 9437184
  96.7 1.6 sort.17
  98.4 3.1 %convolution_convert_fusion.2 = bf16[160,2048]{1,0:T(8,128)(2,1)S(1)} fusion(bf16[2048,768]{1,0:T(8,128)(2,1)} %bitcast.40, bf16[160,384]{1,0:T(8,128)(2,1)} %copy-done.7, bf16[160,384]{1,0:T(8,128)(2,1)S(1)} %copy-done.6), kind=kOutput, calls=%fused_computation.6 | convolution fusion | flops 504135680 | bytes 4046848 | tf_op jit(solution)/shard_map/dot_general | solution.py:94
  102.8 5.2 %all-to-all-start.2 = ((bf16[32,5,2048]{2,1,0:T(8,128)(2,1)}), bf16[32,5,2048]{2,1,0:T(8,128)(2,1)}, u32[]{:S(2)}, u32[]{:S(2)}) async-start(bf16[32,5,2048]{2,1,0:T(8,128)(2,1)} %reshape.74), calls=%async_computation.2 | async-start | bytes 2097152 | tf_op jit(solution)/shard_map/all_to_all | solution.py:97
  108.0 78.9 %reduce-scatter.7.cloned.1.call-done = bf16[128,1152]{1,0:T(8,128)(2,1)} async-done(((bf16[2048,1152]{1,0:T(8,128)(2,1)}), bf16[128,1152]{1,0:T(8,128)(2,1)}) %reduce-scatter.7.cloned.1.call-update) | async-done | bytes 294928
  186.9 1.8 copy.49
  197.8 1.5 gather_fusion.2
  199.3 2.5 gather_fusion.1
  201.8 2.0 multiply_subtract_fusion
  204.8 2.2 broadcast_select_fusion
  207.0 21.3 %all_to_all.30 = bf16[32,4,3,384]{3,1,2,0:T(4,128)(2,1)S(1)} all-to-all(bf16[32,4,3,384]{3,1,2,0:T(4,128)(2,1)S(1)} %get-tuple-element.12), channel_id=1, replica_groups=mesh['expert'=32,'cuts'=2,'dp'=16] {'expert'}, dimensions={0} | all-to-all | bytes 589824 | tf_op jit(solution)/shard_map/all_to_all | solution.py:133
  228.3 4.5 %all-to-all-start.5 = ((bf16[32,4,3,384]{3,1,2,0:T(4,128)(2,1)}), bf16[32,4,3,384]{3,1,2,0:T(4,128)(2,1)S(1)}, u32[]{:S(2)}, u32[]{:S(2)}) async-start(bf16[32,4,3,384]{3,1,2,0:T(4,128)(2,1)} %get-tuple-element.11), calls=%async_computation.6 | async-start | bytes 589824 | tf_op jit(solution)/shard_map/all_to_all | solution.py:140
  232.8 1.5 reshape.75
  235.5 9.3 %all-to-all-done.5 = bf16[32,4,3,384]{3,1,2,0:T(4,128)(2,1)S(1)} async-done(((bf16[32,4,3,384]{3,1,2,0:T(4,128)(2,1)}), bf16[32,4,3,384]{3,1,2,0:T(4,128)(2,1)S(1)}, u32[]{:S(2)}, u32[]{:S(2)}) %all-to-all-start.5) | async-done | bytes 294944 | tf_op jit(solution)/shard_map/all_to_all | solution.py:140
  244.7 5.4 %all-to-all-start.3 = ((bf16[32,4,3,384]{3,1,2,0:T(4,128)(2,1)}), bf16[32,4,3,384]{3,1,2,0:T(4,128)(2,1)S(1)}, u32[]{:S(2)}, u32[]{:S(2)}) async-start(bf16[32,4,3,384]{3,1,2,0:T(4,128)(2,1)} %get-tuple-element.13), calls=%async_computation.4 | async-start | bytes 589824 | tf_op jit(solution)/shard_map/all_to_all | solution.py:129
  250.2 11.4 %all-to-all-done.3 = bf16[32,4,3,384]{3,1,2,0:T(4,128)(2,1)S(1)} async-done(((bf16[32,4,3,384]{3,1,2,0:T(4,128)(2,1)}), bf16[32,4,3,384]{3,1,2,0:T(4,128)(2,1)S(1)}, u32[]{:S(2)}, u32[]{:S(2)}) %all-to-all-start.3) | async-done | bytes 294944 | tf_op jit(solution)/shard_map/all_to_all | solution.py:129
  (62 shorter events, 30.1 us)
Async XLA Ops:
  8.0 72.7 %copy-start = (bf16[1,2048,384]{2,1,0:T(8,128)(2,1)S(1)}, bf16[1,2048,384]{2,1,0:T(8,128)(2,1)}, u32[]{:S(2)}) copy-start(bf16[1,2048,384]{2,1,0:T(8,128)(2,1)} %param.15) | copy-start | bytes 4718596
  13.2 38.7 %all-to-all-start.1 = ((bf16[32,5,2048]{2,1,0:T(8,128)(2,1)}), bf16[32,5,2048]{2,1,0:T(8,128)(2,1)S(1)}, u32[]{:S(2)}, u32[]{:S(2)}) async-start(bf16[32,5,2048]{2,1,0:T(8,128)(2,1)} %reshape.72), calls=%async_computation.1 | async-start | bytes 2097152 | tf_op jit(solution)/shard_map/all_to_all | solution.py:64
  51.9 26.7 %all-to-all-start = ((bf16[32,5,2048]{2,1,0:T(8,128)(2,1)}), bf16[32,5,2048]{2,1,0:T(8,128)(2,1)}, u32[]{:S(2)}, u32[]{:S(2)}) async-start(bf16[32,5,2048]{2,1,0:T(8,128)(2,1)} %reshape.70), calls=%async_computation | async-start | bytes 2097152 | tf_op jit(solution)/shard_map/all_to_all | solution.py:71
  57.1 129.7 %reduce-scatter.7.cloned.1.call-start = ((), (), s32[]{:S(2)}) async-start(), calls=%async_computation.9 | async-start | bytes 5013504
  81.2 1.1 copy-start.5
  81.2 1.1 copy-start.7
  91.6 1.0 copy-start.8
  91.7 3.4 %copy-start.4 = (f32[1,128,3,384]{3,1,2,0:T(8,128)S(1)}, f32[1,128,3,384]{3,1,2,0:T(8,128)}, u32[]{:S(2)}) copy-start(f32[1,128,3,384]{3,1,2,0:T(8,128)} %param.16) | copy-start | bytes 1769476
  91.7 6.7 %copy-start.6 = (bf16[160,384]{1,0:T(8,128)(2,1)S(1)}, bf16[160,384]{1,0:T(8,128)(2,1)}, u32[]{:S(2)}) copy-start(bf16[160,384]{1,0:T(8,128)(2,1)} %copy-done.5) | copy-start | bytes 368644
  92.8 99.3 %copy-start.1 = (f32[32,4,3,384]{3,1,0,2:T(4,128)}, f32[32,4,3,384]{3,1,0,2:T(4,128)S(1)}, u32[]{:S(2)}) copy-start(f32[32,4,3,384]{3,1,0,2:T(4,128)S(1)} %mul.112) | copy-start | bytes 1769476
  102.8 104.2 %all-to-all-start.2 = ((bf16[32,5,2048]{2,1,0:T(8,128)(2,1)}), bf16[32,5,2048]{2,1,0:T(8,128)(2,1)}, u32[]{:S(2)}, u32[]{:S(2)}) async-start(bf16[32,5,2048]{2,1,0:T(8,128)(2,1)} %reshape.74), calls=%async_computation.2 | async-start | bytes 2097152 | tf_op jit(solution)/shard_map/all_to_all | solution.py:97
  194.3 3.5 %copy-start.2 = (bf16[32,4,3,384]{3,1,2,0:T(4,128)(2,1)S(1)}, bf16[32,4,3,384]{3,1,2,0:T(4,128)(2,1)}, u32[]{:S(2)}) copy-start(bf16[32,4,3,384]{3,1,2,0:T(4,128)(2,1)} %copy.47) | copy-start | bytes 884740
  199.3 5.5 %copy-start.3 = (bf16[32,4,3,384]{3,1,2,0:T(4,128)(2,1)S(1)}, bf16[32,4,3,384]{3,1,2,0:T(4,128)(2,1)}, u32[]{:S(2)}) copy-start(bf16[32,4,3,384]{3,1,2,0:T(4,128)(2,1)} %gather_fusion.2) | copy-start | bytes 884740
  228.3 16.5 %all-to-all-start.5 = ((bf16[32,4,3,384]{3,1,2,0:T(4,128)(2,1)}), bf16[32,4,3,384]{3,1,2,0:T(4,128)(2,1)S(1)}, u32[]{:S(2)}, u32[]{:S(2)}) async-start(bf16[32,4,3,384]{3,1,2,0:T(4,128)(2,1)} %get-tuple-element.11), calls=%async_computation.6 | async-start | bytes 589824 | tf_op jit(solution)/shard_map/all_to_all | solution.py:140
  232.8 29.7 %reduce-scatter.5.cloned.1.call-start = ((), (), s32[]{:S(2)}) async-start(), calls=%async_computation.8 | async-start | bytes 786432 | tf_op jit(solution)/shard_map/reduce_scatter | solution.py:110
  244.7 16.8 %all-to-all-start.3 = ((bf16[32,4,3,384]{3,1,2,0:T(4,128)(2,1)}), bf16[32,4,3,384]{3,1,2,0:T(4,128)(2,1)S(1)}, u32[]{:S(2)}, u32[]{:S(2)}) async-start(bf16[32,4,3,384]{3,1,2,0:T(4,128)(2,1)} %get-tuple-element.13), calls=%async_computation.4 | async-start | bytes 589824 | tf_op jit(solution)/shard_map/all_to_all | solution.py:129
Sparse Core Ops, SparseCore 0:
  91.8 95.0 reduce-scatter.6
Sparse Core Ops, SparseCore 1:
  237.2 18.4 reduce-scatter.4
where the time goes:
time: 273 us; the launch traced here: 271 us
  waiting for transfers between devices  133 us (49%)
  starting transfers between devices  37.1 us (14%)
  local copies, waits for them, and re-layouts  36.4 us (13%)
  blocking collectives  21.3 us (8%)
  between operations  15.8 us (6%)
  other arithmetic  15.6 us (6%)
  matrix products  11.8 us (4%)
    unnamed x3, waiting for transfers between devices  78.9 us
    all_to_all x1, blocking collectives, local(): lax.all_to_all(arrange(first_new.astype(jnp.bfloat16)), 'expert', split_a...  21.3 us
    all_to_all x1, waiting for transfers between devices, local(): lax.all_to_all(send_in.reshape(experts, capacity, model_width), 'expert',...  19.5 us
    all_to_all x1, starting transfers between devices, local(): lax.all_to_all(send_in.reshape(experts, capacity, model_width), 'expert',...  16.6 us
    unnamed x23, local copies, waits for them, and re-layouts  15.2 us
    all_to_all x1, waiting for transfers between devices, local(): lax.all_to_all(send_grad.reshape(experts, capacity, model_width), 'expert...  14.4 us
    all_to_all x1, waiting for transfers between devices, local(): lax.all_to_all(arrange(master_new).astype(jnp.bfloat16), 'expert', split_...  11.4 us
    all_to_all x1, waiting for transfers between devices, local(): lax.all_to_all(arrange(second_new.astype(jnp.bfloat16)), 'expert', split_...  9.29 us
  transfers between devices with their start and end apart: 7, of which 5 were waited for; matrix products, arithmetic and copies ran while one was open for 16% of the time, Pallas kernels for 0%

commit v1 on v0

v1 whole, which is shorter than its diff:
```python
import functools

import jax
import jax.numpy as jnp
from jax import lax
from jax.experimental import pallas as pl
from jax.experimental.pallas import tpu as pltpu
from jax.sharding import PartitionSpec as P

beta_first = 0.9
beta_second = 0.95
learn_rate = 0.01
decay_rate = 0.1
epsilon = 1e-08

MESH = pl.DeviceIdType.MESH
LANES = 128
SLOT = 8
F32 = jnp.float32
BF16 = jnp.bfloat16


def one_hot(cond):
    return jnp.where(cond, 1.0, 0.0).astype(BF16)


def dot(a, b):
    return jnp.dot(a, b, preferred_element_type=F32)


def iota(shape, axis):
    return lax.broadcasted_iota(jnp.int32, shape, axis)


def ranks(ids_ref):
    n = ids_ref.shape[1]
    lane = jnp.broadcast_to(ids_ref[...].astype(F32), (n, n))
    sub = lane.T
    same = jnp.where(lane == sub, 1.0, 0.0)
    i, j = iota((n, n), 0), iota((n, n), 1)
    within_lane = jnp.sum(jnp.where(i < j, same, 0.0), axis=0, keepdims=True)
    within_sub = jnp.sum(jnp.where(j < i, same, 0.0), axis=1, keepdims=True)
    return lane[0:1].astype(jnp.int32), within_lane.astype(jnp.int32), sub, within_sub


def dispatch_kernel(
    n_e, ids_ref, act_ref, grad_ref, out_ref, send, ssem, rsem, fssem, frsem, lsem
):
    me, core = lax.axis_index("expert"), lax.axis_index("cuts")
    rows, width = act_ref.shape
    half = width // 2
    total = n_e * SLOT
    sibling = {"cuts": 1 - core}

    barrier = pltpu.get_barrier_semaphore()

    @pl.loop(1, n_e)
    def _(d):
        pl.semaphore_signal(
            barrier, inc=1, device_id={"expert": (me + d) % n_e}, device_id_type=MESH
        )

    pl.semaphore_signal(barrier, inc=1, device_id=sibling, device_id_type=MESH)

    ids, within, _, _ = ranks(ids_ref)
    row = iota((total, rows), 0)
    code_in = ids * SLOT + within
    code_grad = jnp.where(within < 3, ids * SLOT + 5 + within, -1)
    pick = jnp.concatenate([one_hot(row == code_in), one_hot(row == code_grad)], axis=1)
    columns = pl.ds(pl.multiple_of(core * half, half), half)
    both = jnp.concatenate([act_ref[:, columns], grad_ref[:, columns]], axis=0)
    send[:, :half] = dot(pick, both).astype(BF16)
    code_rest = jnp.where(within >= 3, ids * SLOT + within - 3, -1000)
    pick_rest = jnp.concatenate([one_hot(row == code_rest + 2 * l) for l in range(4)], axis=1)
    for u in range(2):
        tiles = [
            both[rows:, (4 * u + l) * LANES : (4 * u + l + 1) * LANES] for l in range(4)
        ]
        send[:, half + u * LANES : half + (u + 1) * LANES] = dot(
            pick_rest, jnp.concatenate(tiles, axis=0)
        ).astype(BF16)

    pl.semaphore_wait(barrier, n_e)

    def block(k):
        return pl.ds(pl.multiple_of(k * SLOT, SLOT), SLOT)

    def out_copy(d):
        return pltpu.make_async_remote_copy(
            src_ref=send.at[block((me + d) % n_e)],
            dst_ref=out_ref.at[core, block(me)],
            send_sem=ssem.at[d],
            recv_sem=rsem.at[d],
            device_id={"expert": (me + d) % n_e},
            device_id_type=MESH,
        )

    def forward(d):
        source = block((me + n_e - d) % n_e)
        return pltpu.make_async_remote_copy(
            src_ref=out_ref.at[core, source],
            dst_ref=out_ref.at[core, source],
            send_sem=fssem.at[d],
            recv_sem=frsem.at[d],
            device_id=sibling,
            device_id_type=MESH,
        )

    def forwarded(d):
        source = block((me + n_e - d) % n_e)
        return pltpu.make_async_remote_copy(
            src_ref=out_ref.at[1 - core, source],
            dst_ref=out_ref.at[1 - core, source],
            send_sem=fssem.at[d],
            recv_sem=frsem.at[d],
            device_id=sibling,
            device_id_type=MESH,
        )

    @pl.loop(1, n_e)
    def _(d):
        out_copy(d).start()

    own = pltpu.make_async_copy(send.at[block(me)], out_ref.at[core, block(me)], lsem)
    own.start()
    own.wait()
    forward(0).start()

    @pl.loop(1, n_e)
    def _(d):
        out_copy(d).wait_recv()
        forward(d).start()

    @pl.loop(0, n_e)
    def _(d):
        forwarded(d).wait_recv()
        forward(d).wait_send()

    @pl.loop(1, n_e)
    def _(d):
        out_copy(d).wait_send()


def expert_kernel(slots_ref, gate_up_ref, down_ref, part_ref, msg_ref, grads, picks, mids, back):
    total, half = slots_ref.shape[1], gate_up_ref.shape[1] // 2
    row = iota((total, total), 0)
    col = iota((total, total), 1)
    place = row % SLOT

    for l in range(4):
        picks[l, :, :total] = one_hot((place < 3) & (col == row + 5))
        picks[l, :, total:] = one_hot(
            ((place == 3) | (place == 4)) & (col == row - 3 + 2 * l)
        )
    for h in range(2):
        for t in range(half // LANES):
            u, l = t // 4, t % 4
            source = jnp.concatenate(
                [
                    slots_ref[h, :, t * LANES : (t + 1) * LANES],
                    slots_ref[h, :, half + u * LANES : half + (u + 1) * LANES],
                ],
                axis=0,
            )
            grads[:, h * half + t * LANES : h * half + (t + 1) * LANES] = dot(
                picks[l], source
            ).astype(BF16)

    first, second = slots_ref[0, :, :half], slots_ref[1, :, :half]
    gate = dot(first, gate_up_ref[0, :half]) + dot(second, gate_up_ref[0, half:])
    lift = dot(first, gate_up_ref[1, :half]) + dot(second, gate_up_ref[1, half:])
    hidden_grad = dot(grads[...], down_ref[...])
    sigmoid_gate = jax.nn.sigmoid(gate)
    silu_gate = gate * sigmoid_gate
    mids[0] = (hidden_grad * lift * sigmoid_gate * (1.0 + gate * (1.0 - sigmoid_gate))).astype(
        BF16
    )
    mids[1] = (hidden_grad * silu_gate).astype(BF16)
    mids[2] = (silu_gate * lift).astype(BF16)

    tile = 256
    over_rows = (((0,), (0,)), ((), ()))
    over_units = (((1,), (1,)), ((), ()))
    for h in range(2):

        @pl.loop(0, half // tile)
        def _(i, h=h):
            at = pl.ds(pl.multiple_of(i * tile, tile), tile)
            wide = pl.ds(pl.multiple_of(h * half + i * tile, tile), tile)
            ins = slots_ref[h, :, at]
            outs = grads[:, wide]
            for g in range(3):
                part_ref[g, wide, :] = lax.dot_general(
                    ins if g < 2 else outs, mids[g], over_rows, preferred_element_type=F32
                ).astype(BF16)
            back[:, wide] = (
                lax.dot_general(
                    mids[0], gate_up_ref[0, wide, :], over_units, preferred_element_type=F32
                )
                + lax.dot_general(
                    mids[1], gate_up_ref[1, wide, :], over_units, preferred_element_type=F32
                )
            ).astype(BF16)

    for m in range(5):
        shift = jnp.concatenate(
            [one_hot((place == 5 + t) & (col == row - 5 - t + m)) for t in range(3)], axis=1
        )
        for h in range(2):
            rest = jnp.concatenate(
                [back[:, h * half + (5 + t) * LANES : h * half + (6 + t) * LANES] for t in range(3)],
                axis=0,
            )
            base = back[:, h * half + m * LANES : h * half + (m + 1) * LANES]
            msg_ref[h, :, m * LANES : (m + 1) * LANES] = (
                base.astype(F32) + dot(shift, rest)
            ).astype(BF16)


def adam_update(master, first_old, second_old, gradient):
    first_new = beta_first * first_old + (1.0 - beta_first) * gradient
    second_new = beta_second * second_old + (1.0 - beta_second) * gradient * gradient
    master_new = master - learn_rate * (
        first_new / (jnp.sqrt(second_new) + epsilon) + decay_rate * master
    )
    return (master_new, first_new, second_new)


def update_kernel(
    n_e,
    n_p,
    part_ref,
    msg_ref,
    ids_ref,
    owner_ref,
    master_ref,
    first_ref,
    second_ref,
    ig_ref,
    moved_ref,
    ring,
    other,
    csend,
    crecv,
    msend,
    ring_s,
    ring_r,
    xsem,
    cs_sem,
    cr_sem,
    ms_sem,
    mr_sem,
    lsem,
):
    me, core, dp = lax.axis_index("expert"), lax.axis_index("cuts"), lax.axis_index("dp")
    shard = master_ref.shape[1]
    hop = shard // 2
    rows = ids_ref.shape[1]
    total = n_e * SLOT
    piece = shard // n_e
    sibling = {"cuts": 1 - core}
    ahead = ({"dp": (dp + 1) % n_p}, {"dp": (dp + n_p - 1) % n_p})

    barrier = pltpu.get_barrier_semaphore()

    @pl.loop(1, n_e)
    def _(d):
        pl.semaphore_signal(
            barrier, inc=1, device_id={"expert": (me + d) % n_e}, device_id_type=MESH
        )

    pl.semaphore_signal(barrier, inc=1, device_id=sibling, device_id_type=MESH)
    for to in ahead:
        pl.semaphore_signal(barrier, inc=1, device_id=to, device_id_type=MESH)
    pl.semaphore_wait(barrier, n_e + 2)

    def own(q, way):
        return pl.ds(pl.multiple_of(q * shard + way * hop, hop), hop)

    def shard_of(t, way):
        return (dp + n_p - 1 - t) % n_p if way == 0 else (dp + 1 + t) % n_p

    def ring_copy(t, g, way, src):
        return pltpu.make_async_remote_copy(
            src_ref=src,
            dst_ref=ring.at[t, g, way],
            send_sem=ring_s.at[t, g, way],
            recv_sem=ring_r.at[t, g, way],
            device_id=ahead[way],
            device_id_type=MESH,
        )

    streams = [(g, way) for g in range(3) for way in range(2)]
    for g, way in streams:
        ring_copy(0, g, way, part_ref.at[g, own(shard_of(0, way), way)]).start()

    swap = pltpu.make_async_remote_copy(
        src_ref=msg_ref.at[1 - core],
        dst_ref=other,
        send_sem=xsem.at[0],
        recv_sem=xsem.at[1],
        device_id=sibling,
        device_id_type=MESH,
    )
    swap.start()
    swap.wait_recv()
    csend[...] = (msg_ref[core].astype(F32) + other[...].astype(F32)).astype(BF16)

    def block(k):
        return pl.ds(pl.multiple_of(k * SLOT, SLOT), SLOT)

    def combine_copy(d):
        return pltpu.make_async_remote_copy(
            src_ref=csend.at[block((me + d) % n_e)],
            dst_ref=crecv.at[block(me)],
            send_sem=cs_sem.at[d],
            recv_sem=cr_sem.at[d],
            device_id={"expert": (me + d) % n_e},
            device_id_type=MESH,
        )

    @pl.loop(1, n_e)
    def _(d):
        combine_copy(d).start()

    keep = pltpu.make_async_copy(csend.at[block(me)], crecv.at[block(me)], lsem.at[0])
    keep.start()

    @pl.loop(1, n_p - 1)
    def _(t):
        for g, way in streams:
            held = ring.at[t - 1, g, way]
            ring_copy(t - 1, g, way, held).wait_recv()
            mine = part_ref[g, own(shard_of(t, way), way), :]
            held[...] = (held[...].astype(F32) + mine.astype(F32)).astype(BF16)
            ring_copy(t, g, way, held).start()

    owners = jnp.where(
        iota((n_e, n_e), 0) == me, owner_ref[...].astype(F32), 0.0
    ).astype(BF16)
    spread = one_hot(iota((n_e, shard), 1) // piece == iota((n_e, shard), 0))
    owner_of = jnp.sum(dot(owners, spread), axis=0, keepdims=True).astype(jnp.int32)
    code = owner_of * SLOT + iota((1, shard), 1) % piece
    arrange = one_hot(iota((total, shard), 0) == code)

    def move_copy(g, d):
        return pltpu.make_async_remote_copy(
            src_ref=msend.at[g, (me + d) % n_e],
            dst_ref=moved_ref.at[me, :, g],
            send_sem=ms_sem.at[g, d],
            recv_sem=mr_sem.at[g, d],
            device_id={"expert": (me + d) % n_e},
            device_id_type=MESH,
        )

    def move_keep(g):
        return pltpu.make_async_copy(
            msend.at[g, me], moved_ref.at[me, :, g], lsem.at[1 + g]
        )

    last = n_p - 2
    for g in range(3):
        sums = []
        for way in range(2):
            held = ring.at[last, g, way]
            ring_copy(last, g, way, held).wait_recv()
            sums.append(held[...].astype(F32) + part_ref[g, own(dp, way), :].astype(F32))
        gradient = jnp.concatenate(sums, axis=0) * (1.0 / n_p)
        new = adam_update(
            master_ref[g], first_ref[g].astype(F32), second_ref[g].astype(F32), gradient
        )
        for k in range(3):
            placed = dot(arrange, new[k].astype(BF16))
            placed = placed.reshape(n_e, SLOT, placed.shape[1])
            msend[g, :, k] = placed[:, :piece].astype(BF16)

        @pl.loop(1, n_e)
        def _(d, g=g):
            move_copy(g, d).start()

        move_keep(g).start()

    keep.wait()

    @pl.loop(1, n_e)
    def _(d):
        combine_copy(d).wait_recv()

    _, _, expert, within = ranks(ids_ref)
    expert = jnp.broadcast_to(expert[:, 0:1], (rows, total)).astype(jnp.int32)
    within = jnp.broadcast_to(within, (rows, total)).astype(jnp.int32)
    col = iota((rows, total), 1)
    ig_ref[:, : 5 * LANES] = dot(
        one_hot(col == expert * SLOT + within), crecv[...]
    ).astype(BF16)
    stacked = jnp.concatenate(
        [crecv[:, m * LANES : (m + 1) * LANES] for m in range(5)], axis=0
    )
    for t in range(3):
        pick = jnp.concatenate(
            [one_hot((col == expert * SLOT + 5 + t) & (within == m)) for m in range(5)], axis=1
        )
        ig_ref[:, (5 + t) * LANES : (6 + t) * LANES] = dot(pick, stacked).astype(BF16)

    swap.wait_send()

    @pl.loop(0, n_p - 1)
    def _(t):
        for g, way in streams:
            ring_copy(t, g, way, ring.at[t, g, way]).wait_send()

    @pl.loop(1, n_e)
    def _(d):
        combine_copy(d).wait_send()

    for g in range(3):
        move_keep(g).wait()

        @pl.loop(1, n_e)
        def _(d, g=g):
            move_copy(g, d).wait_recv()
            move_copy(g, d).wait_send()


VMEM = pl.BlockSpec(memory_space=pltpu.VMEM)


def local(
    activations,
    out_grad,
    expert_ids,
    gate_up_weight,
    down_weight,
    master_weight,
    first_moment,
    second_moment,
    new_owner,
):
    n_e = lax.axis_size("expert")
    n_p = lax.axis_size("dp")
    rows, width = activations.shape
    units = down_weight.shape[2]
    half = width // 2
    total = n_e * SLOT
    shard = width // n_p
    piece = shard // n_e
    ids = expert_ids.reshape(1, rows)
    dma = pltpu.SemaphoreType.DMA

    slots = pl.pallas_call(
        functools.partial(dispatch_kernel, n_e),
        name="dispatch",
        out_shape=jax.ShapeDtypeStruct((2, total, half + 2 * LANES), BF16),
        in_specs=[VMEM] * 3,
        out_specs=VMEM,
        scratch_shapes=[
            pltpu.VMEM((total, half + 2 * LANES), BF16),
            dma((n_e,)),
            dma((n_e,)),
            dma((n_e,)),
            dma((n_e,)),
            dma,
        ],
        compiler_params=pltpu.CompilerParams(collective_id=0, has_side_effects=True),
    )(ids, activations, out_grad)

    gate_up = jnp.moveaxis(gate_up_weight[0], 1, 0)
    part, msg = pl.pallas_call(
        expert_kernel,
        name="expert",
        out_shape=(
            jax.ShapeDtypeStruct((3, width, units), BF16),
            jax.ShapeDtypeStruct((2, total, 5 * LANES), BF16),
        ),
        in_specs=[VMEM] * 3,
        out_specs=(VMEM, VMEM),
        scratch_shapes=[
            pltpu.VMEM((total, width), BF16),
            pltpu.VMEM((4, total, 2 * total), BF16),
            pltpu.VMEM((3, total, units), BF16),
            pltpu.VMEM((total, width), BF16),
        ],
    )(slots, gate_up, down_weight[0])

    input_grad, moved = pl.pallas_call(
        functools.partial(update_kernel, n_e, n_p),
        name="update",
        out_shape=(
            jax.ShapeDtypeStruct((rows, half), BF16),
            jax.ShapeDtypeStruct((n_e, 3, 3, piece, units), BF16),
        ),
        in_specs=[VMEM] * 7,
        out_specs=(VMEM, VMEM),
        scratch_shapes=[
            pltpu.VMEM((n_p - 1, 3, 2, shard // 2, units), BF16),
            pltpu.VMEM((total, 5 * LANES), BF16),
            pltpu.VMEM((total, 5 * LANES), BF16),
            pltpu.VMEM((total, 5 * LANES), BF16),
            pltpu.VMEM((3, n_e, 3, piece, units), BF16),
            dma((n_p - 1, 3, 2)),
            dma((n_p - 1, 3, 2)),
            dma((2,)),
            dma((n_e,)),
            dma((n_e,)),
            dma((3, n_e)),
            dma((3, n_e)),
            dma((4,)),
        ],
        compiler_params=pltpu.CompilerParams(collective_id=1, has_side_effects=True),
    )(
        part,
        msg,
        ids,
        new_owner,
        jnp.moveaxis(master_weight[0], 1, 0),
        jnp.moveaxis(first_moment[0], 1, 0),
        jnp.moveaxis(second_moment[0], 1, 0),
    )
    moved = jnp.moveaxis(moved, 2, 3)
    return (
        input_grad,
        moved[:, 0].astype(F32)[None],
        moved[:, 1][None],
        moved[:, 2][None],
    )


def solution(mesh):
    in_specs = (
        P(("expert", "dp"), None),
        P(("expert", "dp"), None),
        P(("expert", "dp"), None),
        P("expert", None, None, "cuts"),
        P("expert", None, "cuts"),
        P("expert", "dp", None, "cuts"),
        P("expert", "dp", None, "cuts"),
        P("expert", "dp", None, "cuts"),
        P(),
    )
    out_specs = (
        P(("expert", "dp"), "cuts"),
        P("expert", None, "dp", None, "cuts"),
        P("expert", None, "dp", None, "cuts"),
        P("expert", None, "dp", None, "cuts"),
    )
    return jax.shard_map(local, mesh=mesh, in_specs=in_specs, out_specs=out_specs, check_vma=False)
```

time: 273 us -> 146 us (0.53)
  the two profiles are of different devices: /device:TPU:8 before, /device:TPU:32 now
where the time goes in v1:
time: 146 us
  Pallas kernels  137 us (94%)
  local copies, waits for them, and re-layouts  5.63 us (4%)
  other arithmetic  2.34 us (2%)
    pallas_call x1, Pallas kernels, local(): pl.pallas_call(functools.partial(update_kernel, n_e, n_p), name='update',...  96.4 us
    pallas_call x1, Pallas kernels, local(): pl.pallas_call(functools.partial(dispatch_kernel, n_e), name='dispatch',...  28.2 us
    pallas_call x1, Pallas kernels, local(): pl.pallas_call(expert_kernel, name='expert', out_shape=(jax.ShapeDtypeStr...  12.3 us
    unnamed x2, local copies, waits for them, and re-layouts  5.63 us

profile of v1, /device:TPU:32, one launch (start us, length us, event | category | flops | bytes accessed | tf_op | source)
XLA Modules:
  0.0 145.6 jit_solution(10388787370647291725)
XLA Ops:
  0.6 28.2 %dispatch.1.slots_ref = bf16[2,256,1280]{2,1,0:T(8,128)(2,1)} custom-call(s32[1,128]{1,0:T(1,128)} %bitcast.32, bf16[128,2048]{1,0:T(8,128)(2,1)} %act_ref.1, bf16[128,2048]{1,0:T(8,128)(2,1)} %grad_ref.1), custom_call_target="tpu_custom_call" | custom-call | tf_op jit(solution)/shard_map/dispatch/pallas_call | solution.py:450
  28.8 4.0 %copy.15 = bf16[1,2048,2,384]{3,1,2,0:T(8,128)(2,1)} copy(bf16[1,2048,2,384]{3,2,1,0:T(2,128)(2,1)} %param.12) | data formatting | bytes 6291456 | tf_op args[3]
  32.8 12.3 %expert.1 = (bf16[3,2048,384]{2,1,0:T(8,128)(2,1)}, bf16[2,256,640]{2,1,0:T(8,128)(2,1)}) custom-call(bf16[2,256,1280]{2,1,0:T(8,128)(2,1)} %dispatch.1.slots_ref, bf16[2,2048,384]{2,1,0:T(8,128)(2,1)} %bitcast.26, bf16[2048,384]{1,0:T(8,128)(2,1)} %bitcast.27), custom_call_target="tpu_custom_call" | custom-call | tf_op jit(solution)/shard_map/expert/pallas_call | solution.py:468
  45.1 96.4 %update.1 = (bf16[128,1024]{1,0:T(8,128)(2,1)}, bf16[32,3,3,4,384]{4,3,2,1,0:T(4,128)(2,1)}) custom-call(bf16[3,2048,384]{2,1,0:T(8,128)(2,1)} %get-tuple-element.8.part_ref, bf16[2,256,640]{2,1,0:T(8,128)(2,1)} %get-tuple-element.9.msg_ref, s32[1,128]{1,0:T(1,128)} %bitcast.33, s32[32,32]{1,0:T(8,128)} %owner_ref.1, f32[3,128,384]{2,1,0:T(8,128)} %bitcast.29, ...), custom_call_target="tpu_custom_call" | custom-call | tf_op jit(solution)/shard_map/update/pallas_call | solution.py:485
  141.6 2.3 %slice_bitcast_fusion = (bf16[1,32,4,3,384]{4,2,3,1,0:T(4,128)(2,1)}, bf16[1,32,4,3,384]{4,2,3,1,0:T(4,128)(2,1)}, f32[1,32,4,3,384]{4,2,3,1,0:T(4,128)}) fusion(bf16[32,3,4,3,384]{4,2,3,1,0:T(4,128)(2,1)} %bitcast.28), kind=kLoop, calls=%fused_computation.1 | loop fusion | flops 147456 | bytes 2064384 | tf_op jit(solution)/shard_map/broadcast_in_dim;squeeze | solution.py:524
  143.9 1.7 %copy.17 = bf16[128,1024]{1,0:T(8,128)(2,1)} copy(bf16[128,1024]{1,0:T(8,128)(2,1)} %get-tuple-element.19) | data formatting | bytes 524288

commit v2 on v1

v2 whole, which is shorter than its diff:
```python
import functools

import jax
import jax.numpy as jnp
from jax import lax
from jax.experimental import pallas as pl
from jax.experimental.pallas import tpu as pltpu
from jax.sharding import PartitionSpec as P

beta_first = 0.9
beta_second = 0.95
learn_rate = 0.01
decay_rate = 0.1
epsilon = 1e-08

MESH = pl.DeviceIdType.MESH
LANES = 128
SLOT = 8
F32 = jnp.float32
BF16 = jnp.bfloat16


def one_hot(cond):
    return jnp.where(cond, 1.0, 0.0).astype(BF16)


def dot(a, b):
    return jnp.dot(a, b, preferred_element_type=F32)


def iota(shape, axis):
    return lax.broadcasted_iota(jnp.int32, shape, axis)


def ranks(ids_ref):
    n = ids_ref.shape[1]
    lane = jnp.broadcast_to(ids_ref[...].astype(F32), (n, n))
    sub = lane.T
    same = jnp.where(lane == sub, 1.0, 0.0)
    i, j = iota((n, n), 0), iota((n, n), 1)
    within_lane = jnp.sum(jnp.where(i < j, same, 0.0), axis=0, keepdims=True)
    within_sub = jnp.sum(jnp.where(j < i, same, 0.0), axis=1, keepdims=True)
    return lane[0:1].astype(jnp.int32), within_lane.astype(jnp.int32), sub, within_sub


def adam_update(master, first_old, second_old, gradient):
    first_new = beta_first * first_old + (1.0 - beta_first) * gradient
    second_new = beta_second * second_old + (1.0 - beta_second) * gradient * gradient
    master_new = master - learn_rate * (
        first_new / (jnp.sqrt(second_new) + epsilon) + decay_rate * master
    )
    return (master_new, first_new, second_new)


STAGGER = 2


def step_kernel(
    n_e,
    n_p,
    ids_ref,
    owner_ref,
    act_any,
    grad_any,
    gate_up_any,
    down_any,
    master_any,
    first_any,
    second_any,
    ig_ref,
    moved_ref,
    act,
    grad,
    raw,
    gate_up,
    down,
    master,
    first,
    second,
    send,
    slots,
    grads,
    picks,
    mids,
    back,
    msg,
    parts,
    begin,
    ring,
    other,
    csend,
    crecv,
    place_ref,
    msend,
    load_sem,
    keep_sem,
    ssem,
    rsem,
    fssem,
    frsem,
    ring_s,
    ring_r,
    xsem,
    cs_sem,
    cr_sem,
    ms_sem,
    mr_sem,
):
    me, core, dp = lax.axis_index("expert"), lax.axis_index("cuts"), lax.axis_index("dp")
    rows, half = act.shape
    width = 2 * half
    total = n_e * SLOT
    shard = master.shape[1]
    hop = shard // 2
    piece = shard // n_e
    per_half = half // shard
    sibling = {"cuts": 1 - core}
    ahead = ({"dp": (dp + 1) % n_p}, {"dp": (dp + n_p - 1) % n_p})

    def peer(d):
        return (me + d) % n_e

    def block(k):
        return pl.ds(pl.multiple_of(k * SLOT, SLOT), SLOT)

    columns = pl.ds(pl.multiple_of(core * half, half), half)
    loads = [
        pltpu.make_async_copy(src, dst, load_sem.at[i])
        for i, (src, dst) in enumerate(
            (
                (act_any.at[:, columns], act),
                (grad_any.at[:, columns], grad),
                (gate_up_any, raw),
                (down_any, down),
                (master_any, master),
                (first_any, first),
                (second_any, second),
            )
        )
    ]
    for load in loads:
        load.start()

    barrier = pltpu.get_barrier_semaphore()

    @pl.loop(1, n_e)
    def _(d):
        pl.semaphore_signal(
            barrier, inc=1, device_id={"expert": peer(d)}, device_id_type=MESH
        )

    for to in (sibling, *ahead):
        pl.semaphore_signal(barrier, inc=1, device_id=to, device_id_type=MESH)

    ids, within, _, _ = ranks(ids_ref)
    row = iota((total, rows), 0)
    code_in = ids * SLOT + within
    code_grad = jnp.where(within < 3, ids * SLOT + 5 + within, -1)
    pick = jnp.concatenate([one_hot(row == code_in), one_hot(row == code_grad)], axis=1)
    code_rest = jnp.where(within >= 3, ids * SLOT + within - 3, -1000)
    pick_rest = jnp.concatenate([one_hot(row == code_rest + 2 * l) for l in range(4)], axis=1)
    loads[0].wait()
    loads[1].wait()
    send[:, :half] = dot(pick, jnp.concatenate([act[...], grad[...]], axis=0)).astype(BF16)
    for u in range(2):
        tiles = [grad[:, (4 * u + l) * LANES : (4 * u + l + 1) * LANES] for l in range(4)]
        send[:, half + u * LANES : half + (u + 1) * LANES] = dot(
            pick_rest, jnp.concatenate(tiles, axis=0)
        ).astype(BF16)

    pl.semaphore_wait(barrier, n_e + 2)

    def out_copy(d):
        return pltpu.make_async_remote_copy(
            src_ref=send.at[block(peer(d))],
            dst_ref=slots.at[core, block(me)],
            send_sem=ssem.at[d],
            recv_sem=rsem.at[d],
            device_id={"expert": peer(d)},
            device_id_type=MESH,
        )

    def forward(d, from_core):
        at = slots.at[from_core, block((me + n_e - d) % n_e)]
        return pltpu.make_async_remote_copy(
            src_ref=at,
            dst_ref=at,
            send_sem=fssem.at[d],
            recv_sem=frsem.at[d],
            device_id=sibling,
            device_id_type=MESH,
        )

    @pl.loop(1, n_e)
    def _(d):
        out_copy(d).start()

    own = pltpu.make_async_copy(send.at[block(me)], slots.at[core, block(me)], keep_sem.at[0])
    own.start()
    own.wait()
    forward(0, core).start()

    loads[2].wait()
    lines = 256

    @pl.loop(0, width // lines)
    def _(i):
        at = pl.ds(pl.multiple_of(i * lines, lines), lines)
        gate_up[:, at, :] = jnp.swapaxes(raw[at], 0, 1)

    row2 = iota((total, total), 0)
    col2 = iota((total, total), 1)
    place = row2 % SLOT
    for l in range(4):
        picks[l, :, :total] = one_hot((place < 3) & (col2 == row2 + 5))
        picks[l, :, total:] = one_hot(
            ((place == 3) | (place == 4)) & (col2 == row2 - 3 + 2 * l)
        )
    owners = jnp.where(
        iota((n_e, n_e), 0) == me, owner_ref[...].astype(F32), 0.0
    ).astype(BF16)
    spread = one_hot(iota((n_e, shard), 1) // piece == iota((n_e, shard), 0))
    owner_of = jnp.sum(dot(owners, spread), axis=0, keepdims=True).astype(jnp.int32)
    code = owner_of * SLOT + iota((1, shard), 1) % piece
    place_ref[...] = one_hot(iota((total, shard), 0) == code)
    for load in loads[3:]:
        load.wait()

    @pl.loop(1, n_e)
    def _(d):
        out_copy(d).wait_recv()
        forward(d, core).start()

    @pl.loop(0, n_e)
    def _(d):
        forward(d, 1 - core).wait_recv()

    for h in range(2):
        for t in range(half // LANES):
            u, l = t // 4, t % 4
            source = jnp.concatenate(
                [
                    slots[h, :, t * LANES : (t + 1) * LANES],
                    slots[h, :, half + u * LANES : half + (u + 1) * LANES],
                ],
                axis=0,
            )
            grads[:, h * half + t * LANES : h * half + (t + 1) * LANES] = dot(
                picks[l], source
            ).astype(BF16)
    low, high = slots[0, :, :half], slots[1, :, :half]
    gate = dot(low, gate_up[0, :half]) + dot(high, gate_up[0, half:])
    lift = dot(low, gate_up[1, :half]) + dot(high, gate_up[1, half:])
    hidden_grad = dot(grads[...], down[...])
    sigmoid_gate = jax.nn.sigmoid(gate)
    silu_gate = gate * sigmoid_gate
    mids[0] = (hidden_grad * lift * sigmoid_gate * (1.0 + gate * (1.0 - sigmoid_gate))).astype(
        BF16
    )
    mids[1] = (hidden_grad * silu_gate).astype(BF16)
    mids[2] = (silu_gate * lift).astype(BF16)

    def shard_of(t, way):
        return (dp + n_p - 1 - t) % n_p if way == 0 else (dp + 1 + t) % n_p

    def share(g, q, way):
        if g < 2:
            at = pl.ds(pl.multiple_of((q % per_half) * shard, shard), shard)
            lhs = slots[q // per_half, :, at]
        else:
            lhs = grads[:, pl.ds(pl.multiple_of(q * shard, shard), shard)]
        return dot(lhs.T[way * hop : (way + 1) * hop], mids[g])

    def ring_copy(t, g, way, src):
        return pltpu.make_async_remote_copy(
            src_ref=src,
            dst_ref=ring.at[t, g, way],
            send_sem=ring_s.at[t, g, way],
            recv_sem=ring_r.at[t, g, way],
            device_id=ahead[way],
            device_id_type=MESH,
        )

    def ring_start(g):
        for way in range(2):
            begin[g, way] = share(g, shard_of(0, way), way).astype(BF16)
            ring_copy(0, g, way, begin.at[g, way]).start()

    def ring_step(step, active, extra):
        for g in active:
            for way in range(2):
                parts[g, way] = share(g, shard_of(step - g * STAGGER, way), way)
        if extra is not None:
            extra(step)
        for g in active:
            for way in range(2):
                t = step - g * STAGGER
                held = ring.at[t - 1, g, way]
                ring_copy(t - 1, g, way, held).wait_recv()
                held[...] = (held[...].astype(F32) + parts[g, way]).astype(BF16)
                ring_copy(t, g, way, held).start()

    tile = 256
    over_units = (((1,), (1,)), ((), ()))

    def rows_back(step):
        for j in range(2):
            wide = pl.ds(pl.multiple_of((step - 1) * (2 * tile) + j * tile, tile), tile)
            back[:, wide] = (
                lax.dot_general(
                    mids[0], gate_up[0, wide, :], over_units, preferred_element_type=F32
                )
                + lax.dot_general(
                    mids[1], gate_up[1, wide, :], over_units, preferred_element_type=F32
                )
            ).astype(BF16)

    back_steps = width // (2 * tile)

    def pack_back(step):
        m = step - 1 - back_steps
        shift = jnp.concatenate(
            [one_hot((place == 5 + t) & (col2 == row2 - 5 - t + m)) for t in range(3)], axis=1
        )
        for h in range(2):
            rest = jnp.concatenate(
                [back[:, h * half + (5 + t) * LANES : h * half + (6 + t) * LANES] for t in range(3)],
                axis=0,
            )
            base = back[:, pl.ds(pl.multiple_of(h * half + m * LANES, LANES), LANES)]
            msg[h, :, pl.ds(pl.multiple_of(m * LANES, LANES), LANES)] = (
                base.astype(F32) + dot(shift, rest)
            ).astype(BF16)

    swap = pltpu.make_async_remote_copy(
        src_ref=msg.at[1 - core],
        dst_ref=other,
        send_sem=xsem.at[0],
        recv_sem=xsem.at[1],
        device_id=sibling,
        device_id_type=MESH,
    )

    def combine_copy(d):
        return pltpu.make_async_remote_copy(
            src_ref=csend.at[block(peer(d))],
            dst_ref=crecv.at[block(me)],
            send_sem=cs_sem.at[d],
            recv_sem=cr_sem.at[d],
            device_id={"expert": peer(d)},
            device_id_type=MESH,
        )

    keep = pltpu.make_async_copy(csend.at[block(me)], crecv.at[block(me)], keep_sem.at[1])

    def combine(step):
        swap.wait_recv()
        csend[...] = (msg[core].astype(F32) + other[...].astype(F32)).astype(BF16)

        @pl.loop(1, n_e)
        def _(d):
            combine_copy(d).start()

        keep.start()

    def move_copy(g, d):
        return pltpu.make_async_remote_copy(
            src_ref=msend.at[g, peer(d)],
            dst_ref=moved_ref.at[me, :, g],
            send_sem=ms_sem.at[g, d],
            recv_sem=mr_sem.at[g, d],
            device_id={"expert": peer(d)},
            device_id_type=MESH,
        )

    def move_keep(g):
        return pltpu.make_async_copy(
            msend.at[g, me], moved_ref.at[me, :, g], keep_sem.at[2 + g]
        )

    last = n_p - 2

    def finish(g):
        sums = []
        for way in range(2):
            held = ring.at[last, g, way]
            ring_copy(last, g, way, held).wait_recv()
            sums.append(held[...].astype(F32) + parts[g, way])
        gradient = jnp.concatenate(sums, axis=0) * (1.0 / n_p)
        new = adam_update(
            master[g], first[g].astype(F32), second[g].astype(F32), gradient
        )
        for k in range(3):
            placed = dot(place_ref[...], new[k].astype(BF16))
            placed = placed.reshape(n_e, SLOT, placed.shape[1])
            msend[g, :, k] = placed[:, :piece].astype(BF16)

        @pl.loop(1, n_e)
        def _(d):
            move_copy(g, d).start()

        move_keep(g).start()

    def plan(step):
        starts = tuple(g for g in range(3) if step == g * STAGGER)
        active = tuple(g for g in range(3) if 1 <= step - g * STAGGER <= last)
        ends = tuple(g for g in range(3) if step - g * STAGGER == last + 1)
        if 1 <= step <= back_steps:
            extra = rows_back
        elif back_steps < step <= back_steps + 5:
            extra = pack_back
        else:
            extra = None
        return starts, active, ends, extra

    swap_at = back_steps + 6
    step, stop = 0, last + 2 + 2 * STAGGER
    while step < stop:
        starts, active, ends, extra = plan(step)
        if step == swap_at:
            swap.start()
        if step == swap_at + 1:
            extra = combine
        special = starts or ends or step in (swap_at, swap_at + 1)
        until = step + 1
        while not special and until < stop and until not in (swap_at, swap_at + 1):
            if plan(until) != (starts, active, ends, extra):
                break
            until += 1
        if until - step > 1:

            @pl.loop(step, until)
            def _(s, active=active, extra=extra):
                ring_step(s, active, extra)

        else:
            ring_step(step, active, extra)
        for g in starts:
            ring_start(g)
        for g in ends:
            for way in range(2):
                parts[g, way] = share(g, dp, way)
            finish(g)
        step = until

    keep.wait()

    @pl.loop(1, n_e)
    def _(d):
        combine_copy(d).wait_recv()

    _, _, expert, within = ranks(ids_ref)
    expert = jnp.broadcast_to(expert[:, 0:1], (rows, total)).astype(jnp.int32)
    within = jnp.broadcast_to(within, (rows, total)).astype(jnp.int32)
    col = iota((rows, total), 1)
    ig_ref[:, : 5 * LANES] = dot(
        one_hot(col == expert * SLOT + within), crecv[...]
    ).astype(BF16)
    stacked = jnp.concatenate(
        [crecv[:, m * LANES : (m + 1) * LANES] for m in range(5)], axis=0
    )
    for t in range(3):
        pick = jnp.concatenate(
            [one_hot((col == expert * SLOT + 5 + t) & (within == m)) for m in range(5)], axis=1
        )
        ig_ref[:, (5 + t) * LANES : (6 + t) * LANES] = dot(pick, stacked).astype(BF16)

    swap.wait_send()

    @pl.loop(1, n_e)
    def _(d):
        out_copy(d).wait_send()
        combine_copy(d).wait_send()

    @pl.loop(0, n_e)
    def _(d):
        forward(d, core).wait_send()

    @pl.loop(0, n_p - 1)
    def _(t):
        for g in range(3):
            for way in range(2):
                ring_copy(t, g, way, ring.at[t, g, way]).wait_send()

    for g in range(3):
        move_keep(g).wait()

        @pl.loop(1, n_e)
        def _(d, g=g):
            move_copy(g, d).wait_recv()
            move_copy(g, d).wait_send()


VMEM = pl.BlockSpec(memory_space=pltpu.VMEM)
ANY = pl.BlockSpec(memory_space=pl.ANY)


def local(
    activations,
    out_grad,
    expert_ids,
    gate_up_weight,
    down_weight,
    master_weight,
    first_moment,
    second_moment,
    new_owner,
):
    n_e = lax.axis_size("expert")
    n_p = lax.axis_size("dp")
    rows, width = activations.shape
    units = down_weight.shape[2]
    half = width // 2
    total = n_e * SLOT
    shard = width // n_p
    piece = shard // n_e
    line = half + 2 * LANES
    dma = pltpu.SemaphoreType.DMA

    def vmem(*shape, dtype=BF16):
        return pltpu.VMEM(shape, dtype)

    input_grad, moved = pl.pallas_call(
        functools.partial(step_kernel, n_e, n_p),
        name="step",
        out_shape=(
            jax.ShapeDtypeStruct((rows, half), BF16),
            jax.ShapeDtypeStruct((n_e, 3, 3, piece, units), BF16),
        ),
        in_specs=[VMEM] * 2 + [ANY] * 7,
        out_specs=(VMEM, VMEM),
        scratch_shapes=[
            vmem(rows, half),
            vmem(rows, half),
            vmem(width, 2, units),
            vmem(2, width, units),
            vmem(width, units),
            vmem(3, shard, units, dtype=F32),
            vmem(3, shard, units),
            vmem(3, shard, units),
            vmem(total, line),
            vmem(2, total, line),
            vmem(total, width),
            vmem(4, total, 2 * total),
            vmem(3, total, units),
            vmem(total, width),
            vmem(2, total, 5 * LANES),
            vmem(3, 2, shard // 2, units, dtype=F32),
            vmem(3, 2, shard // 2, units),
            vmem(n_p - 1, 3, 2, shard // 2, units),
            vmem(total, 5 * LANES),
            vmem(total, 5 * LANES),
            vmem(total, 5 * LANES),
            vmem(total, shard),
            vmem(3, n_e, 3, piece, units),
            dma((7,)),
            dma((5,)),
            dma((n_e,)),
            dma((n_e,)),
            dma((n_e,)),
            dma((n_e,)),
            dma((n_p - 1, 3, 2)),
            dma((n_p - 1, 3, 2)),
            dma((2,)),
            dma((n_e,)),
            dma((n_e,)),
            dma((3, n_e)),
            dma((3, n_e)),
        ],
        compiler_params=pltpu.CompilerParams(collective_id=0, has_side_effects=True),
    )(
        expert_ids.reshape(1, rows),
        new_owner,
        activations,
        out_grad,
        gate_up_weight[0],
        down_weight[0],
        jnp.moveaxis(master_weight[0], 1, 0),
        jnp.moveaxis(first_moment[0], 1, 0),
        jnp.moveaxis(second_moment[0], 1, 0),
    )
    moved = jnp.moveaxis(moved, 2, 3)
    return (
        input_grad,
        moved[:, 0].astype(F32)[None],
        moved[:, 1][None],
        moved[:, 2][None],
    )


def solution(mesh):
    in_specs = (
        P(("expert", "dp"), None),
        P(("expert", "dp"), None),
        P(("expert", "dp"), None),
        P("expert", None, None, "cuts"),
        P("expert", None, "cuts"),
        P("expert", "dp", None, "cuts"),
        P("expert", "dp", None, "cuts"),
        P("expert", "dp", None, "cuts"),
        P(),
    )
    out_specs = (
        P(("expert", "dp"), "cuts"),
        P("expert", None, "dp", None, "cuts"),
        P("expert", None, "dp", None, "cuts"),
        P("expert", None, "dp", None, "cuts"),
    )
    return jax.shard_map(local, mesh=mesh, in_specs=in_specs, out_specs=out_specs, check_vma=False)
```

time: 146 us -> 133 us (0.911)
  the two profiles are of different devices: /device:TPU:32 before, /device:TPU:2 now
where the time goes in v2:
time: 133 us; the launch traced here: 132 us
  Pallas kernels  128 us (96%)
  other arithmetic  2.34 us (2%)
  local copies, waits for them, and re-layouts  1.67 us (1%)
    pallas_call x1, Pallas kernels, local(): pl.pallas_call(functools.partial(step_kernel, n_e, n_p), name='step', out...  128 us

profile of v2, /device:TPU:2, one launch (start us, length us, event | category | flops | bytes accessed | tf_op | source)
XLA Modules:
  0.0 132.3 jit_solution(9085054106195823231)
XLA Ops:
  0.6 127.6 %step.1 = (bf16[128,1024]{1,0:T(8,128)(2,1)}, bf16[32,3,3,4,384]{4,3,2,1,0:T(4,128)(2,1)}) custom-call(s32[1,128]{1,0:T(1,128)} %bitcast.28, s32[32,32]{1,0:T(8,128)} %owner_ref.1, bf16[128,2048]{1,0:T(8,128)(2,1)} %act_any.1, bf16[128,2048]{1,0:T(8,128)(2,1)} %grad_any.1, bf16[2048,2,384]{2,1,0:T(2,128)(2,1)} %bitcast.22, bf16[2048,384]{1,0:T(8,128)(2,1)} %bitcast.23, ...), custom_call_target="tpu_custom_call" | custom-call | tf_op jit(solution)/shard_map/step/pallas_call | solution.py:523
  128.3 2.3 %slice_bitcast_fusion = (bf16[1,32,4,3,384]{4,2,3,1,0:T(4,128)(2,1)}, bf16[1,32,4,3,384]{4,2,3,1,0:T(4,128)(2,1)}, f32[1,32,4,3,384]{4,2,3,1,0:T(4,128)}) fusion(bf16[32,3,4,3,384]{4,2,3,1,0:T(4,128)(2,1)} %bitcast.24), kind=kLoop, calls=%fused_computation | loop fusion | flops 147456 | bytes 2064384 | tf_op jit(solution)/shard_map/broadcast_in_dim;squeeze | solution.py:587
  130.6 1.7 %copy.14 = bf16[128,1024]{1,0:T(8,128)(2,1)} copy(bf16[128,1024]{1,0:T(8,128)(2,1)} %get-tuple-element.15) | data formatting | bytes 524288

commit v3 on v2

--- a/solution.py
+++ b/solution.py
@@ -52,7 +52,7 @@
     return (master_new, first_new, second_new)
 
 
-STAGGER = 2
+STAGGER = 0
 
 
 def step_kernel(
@@ -491,6 +491,13 @@
             move_copy(g, d).wait_send()
 
 
+def deliver_kernel(ig_in, moved_ref, ig_ref, master_ref, first_ref, second_ref):
+    ig_ref[...] = ig_in[...]
+    master_ref[...] = moved_ref[:, 0].astype(F32)
+    first_ref[...] = moved_ref[:, 1]
+    second_ref[...] = moved_ref[:, 2]
+
+
 VMEM = pl.BlockSpec(memory_space=pltpu.VMEM)
 ANY = pl.BlockSpec(memory_space=pl.ANY)
 
@@ -579,13 +586,20 @@
         jnp.moveaxis(first_moment[0], 1, 0),
         jnp.moveaxis(second_moment[0], 1, 0),
     )
-    moved = jnp.moveaxis(moved, 2, 3)
-    return (
-        input_grad,
-        moved[:, 0].astype(F32)[None],
-        moved[:, 1][None],
-        moved[:, 2][None],
-    )
+    block = (n_e, 3, piece, units)
+    input_grad, *moved = pl.pallas_call(
+        deliver_kernel,
+        name="deliver",
+        out_shape=(
+            jax.ShapeDtypeStruct((rows, half), BF16),
+            jax.ShapeDtypeStruct(block, F32),
+            jax.ShapeDtypeStruct(block, BF16),
+            jax.ShapeDtypeStruct(block, BF16),
+        ),
+        in_specs=[VMEM] * 2,
+        out_specs=(VMEM,) * 4,
+    )(input_grad, moved)
+    return (input_grad, *(jnp.moveaxis(array, 1, 2)[None] for array in moved))
 
 
 def solution(mesh):

time: 133 us -> 128 us (0.962)
  other arithmetic: 2.34 us -> 0 us
  local copies, waits for them, and re-layouts: 1.67 us -> 0 us
    pallas_call x1, Pallas kernels: 128 us -> 125 us  [local(): pl.pallas_call(functools.partial(step_kernel, n_e, n_p), name='step', out...]
    pallas_call x0 -> x1, Pallas kernels: none -> 2.41 us  [local(): pl.pallas_call(deliver_kernel, name='deliver', out_shape=(jax.ShapeDtypeS...]
    another operation x1 -> x0, other arithmetic: 2.34 us -> none  [local(): moved[:, 2][None]]
    unnamed x1 -> x0, local copies, waits for them, and re-layouts: 1.67 us -> none
where the time goes in v3:
time: 128 us
  Pallas kernels  127 us (99%)
    pallas_call x1, Pallas kernels, local(): pl.pallas_call(functools.partial(step_kernel, n_e, n_p), name='step', out...  125 us

profile of v3, /device:TPU:2, one launch (start us, length us, event | category | flops | bytes accessed | tf_op | source)
XLA Modules:
  0.0 127.7 jit_solution(9959813279627241524)
XLA Ops:
  0.6 124.7 %step.1 = (bf16[128,1024]{1,0:T(8,128)(2,1)}, bf16[32,3,3,4,384]{4,3,2,1,0:T(4,128)(2,1)}) custom-call(s32[1,128]{1,0:T(1,128)} %bitcast.26, s32[32,32]{1,0:T(8,128)} %owner_ref.1, bf16[128,2048]{1,0:T(8,128)(2,1)} %act_any.1, bf16[128,2048]{1,0:T(8,128)(2,1)} %grad_any.1, bf16[2048,2,384]{2,1,0:T(2,128)(2,1)} %bitcast.21, bf16[2048,384]{1,0:T(8,128)(2,1)} %bitcast.22, ...), custom_call_target="tpu_custom_call" | custom-call | tf_op jit(solution)/shard_map/step/pallas_call | solution.py:530
  125.3 2.4 %deliver.1 = (bf16[128,1024]{1,0:T(8,128)(2,1)}, f32[32,3,4,384]{3,2,1,0:T(4,128)}, bf16[32,3,4,384]{3,2,1,0:T(4,128)(2,1)}, bf16[32,3,4,384]{3,2,1,0:T(4,128)(2,1)}) custom-call(bf16[128,1024]{1,0:T(8,128)(2,1)} %get-tuple-element.10.ig_in, bf16[32,3,3,4,384]{4,3,2,1,0:T(4,128)(2,1)} %get-tuple-element.11.moved_ref), custom_call_target="tpu_custom_call" | custom-call | tf_op jit(solution)/shard_map/deliver/pallas_call | solution.py:590
